TPU v7x, 32 devices: a whole 2x2x4 slice. The times are simulated.
32 devices in a mesh: dp: 16 (over z, y, x), blk: 2 (over core).
Axes of the slice: x: 2, y: 2, z: 4, core: 2. Of those that a mesh axis runs over, the one named last changes fastest.
Arguments:
- vectors: float32 [16384, 96], P('dp'), may hold values from -16 to 16
- codes: int32 [16384, 8], P('dp'), may hold values from 0 to 255, as said below
- weights: bfloat16 [16384], P('dp'), may hold values from 0.25 to 4
- ridge: float32 [1], replicated, may hold values from 0.1 to 0.5
Outputs:
- codebooks: float32 [8, 256, 96], replicated
- residual: float32 [16384, 96], P('dp')
- distortion: float32 [], replicated
Inputs may be any that keep to these rules, and one draw needn't show every extreme that they name: `codes`: 8 codebook indices per vector.
All inputs are finite; a program needn't handle non-finite values.
Results may differ from a plain program's by a relative error of at most 0.0003.
Values sent between devices are 32-bit elements; how exact they have to be, the bound alone decides.
A program may use at most 128 MiB of HBM per device.

v0:
```python
import functools

import jax
import jax.numpy as jnp
from jax import lax
from jax.experimental import pallas as pl
from jax.experimental.pallas import tpu as pltpu
from jax.sharding import PartitionSpec as P

K = 256
M = 8
ITERS = 8
MESH = pl.DeviceIdType.MESH
HIGH = lax.Precision.HIGHEST
F32 = jnp.float32
BF16 = jnp.bfloat16
NT = (((1,), (1,)), ((), ()))


def vmem():
    return pl.BlockSpec(memory_space=pltpu.VMEM)


def split2(value):
    high = value.astype(BF16)
    low = (value - high.astype(F32)).astype(BF16)
    return high, low


def split3(value):
    high = value.astype(BF16)
    rest = value - high.astype(F32)
    middle = rest.astype(BF16)
    low = (rest - middle.astype(F32)).astype(BF16)
    return high, middle, low


def column_groups(groups, width):
    best = 1
    for count in range(1, groups + 1):
        if groups % count == 0 and width % count == 0 and (width // count) % 8 == 0:
            best = count
    return best


def hot_t(row, levels):
    return jnp.where(levels == row, jnp.ones((), BF16), jnp.zeros((), BF16))


def flip(value, mask, size):
    total, digit = 0, 1
    while digit < size:
        total = total + digit * lax.rem(value // digit + mask // digit % 2, 2)
        digit *= 2
    return total


def column(pieces):
    total = pieces[0]
    for piece in pieces[1:]:
        total = total + piece
    return jnp.sum(total, axis=1, keepdims=True)


def kernel(n, nblk, ncg, ridge_ref, codes_ref, mass_ref, vectors_ref, book_out, residual_out, sum_out,
           codes_all, mass_all, part, pieces, gram, halves, swap, solution, remain, direction, inverse,
           books, parts, gathered, send_sem, recv_sem, swap_send, swap_recv, far_send, far_recv,
           near_send, near_recv, sum_send, sum_recv):
    width, rows = vectors_ref.shape
    gsz = M // nblk
    cols = width // ncg
    me = lax.axis_index("dp")
    blk = lax.axis_index("blk")
    group, member = me // gsz, lax.rem(me, gsz)
    book = nblk * member + blk
    mine = lax.rem(group, ncg)
    bases = group - mine
    half = M // nblk
    peers = [(dm, db) for dm in range(gsz - 1, -1, -1) for db in range(nblk - 1, -1, -1) if (dm, db) != (0, 0)]

    def chip(k):
        return {"dp": lax.rem(me + k, n)}

    def team(dm, db):
        return {"dp": group * gsz + flip(member, dm, gsz), "blk": lax.rem(blk + db, nblk)}

    def far(k):
        return {"dp": (bases + lax.rem(mine + k, ncg)) * gsz + member, "blk": blk}

    def remote(source, target, send, recv, to):
        return pltpu.make_async_remote_copy(
            src_ref=source, dst_ref=target, send_sem=send, recv_sem=recv, device_id=to, device_id_type=MESH
        )

    def loop(function):
        def step(k, carry):
            function(k)
            return carry

        lax.fori_loop(1, n, step, 0)

    barrier = pltpu.get_barrier_semaphore()
    loop(lambda k: pl.semaphore_signal(barrier, inc=1, device_id=chip(k), device_id_type=MESH))
    others = [(dm, db) for dm, db in peers if db]
    for dm, db in others:
        pl.semaphore_signal(barrier, inc=1, device_id=team(dm, db), device_id_type=MESH)

    triple = jnp.concatenate(split3(vectors_ref[...]), axis=0)
    levels = lax.broadcasted_iota(jnp.int32, (K, rows), 0).astype(F32).astype(BF16)

    def spread(row, mass):
        return jnp.where(levels == row.astype(F32).astype(BF16), jnp.broadcast_to(mass, (K, rows)), jnp.zeros((), BF16))

    for m in range(gsz):
        hot = spread(codes_ref[pl.ds(nblk * m + blk, 1), :], mass_ref[...].astype(BF16))
        sums = lax.dot_general(triple, hot, NT, preferred_element_type=F32)
        total = sums[:width] + sums[width : 2 * width] + sums[2 * width :]
        for c in range(ncg):
            part[c, m] = total[c * cols : (c + 1) * cols]
    pl.semaphore_wait(barrier, n - 1 + len(others))

    def codes_copy(k):
        return remote(codes_ref, codes_all.at[me], send_sem.at[0, k], recv_sem.at[0, k], chip(k))

    def mass_copy(k):
        return remote(mass_ref, mass_all.at[me], send_sem.at[1, k], recv_sem.at[1, k], chip(k))

    def piece_copy(k):
        to = lax.rem(me + k, n)
        piece = part.at[lax.rem(to // gsz, ncg), lax.rem(to, gsz)]
        return remote(piece, pieces.at[me], send_sem.at[2, k], recv_sem.at[2, k], chip(k))

    def send_codes(k):
        codes_copy(k).start()
        mass_copy(k).start()

    loop(send_codes)

    codes_all[me] = codes_ref[...]
    mass_all[me] = mass_ref[...]
    pieces[me] = part[mine, member]
    gram[...] = jnp.zeros_like(gram)

    def block(q):
        return pl.ds(pl.multiple_of(q * K, K), K)

    def accumulate(source):
        weighted = spread(codes_all[source, pl.ds(book, 1), :], mass_all[source].astype(BF16))
        for j in range(1, M):
            other = lax.rem(book + j, M)
            hot = spread(codes_all[source, pl.ds(other, 1), :], jnp.ones((1, 1), BF16))
            gram[block(other), :] += lax.dot_general(hot, weighted, NT, preferred_element_type=F32)

    accumulate(me)

    def arrive(k):
        codes_copy(k).wait_recv()
        mass_copy(k).wait_recv()
        piece_copy(k).start()
        accumulate(lax.rem(me - k + n, n))

    loop(arrive)

    square = (K, K)
    own = jnp.sum(gram[block(lax.rem(book + 1, M)), :], axis=0, keepdims=True)
    diagonal = lax.broadcasted_iota(jnp.int32, square, 0) == lax.broadcasted_iota(jnp.int32, square, 1)
    gram[block(book), :] = jnp.where(diagonal, jnp.broadcast_to(own, square), 0.0)
    ones = jnp.ones((8, K), F32)
    for q in range(M):
        value = gram[block(q), :]
        high, low = split2(value)
        halves[block(q), :K] = high
        halves[block(q), K:] = low
        inverse[q] = lax.dot_general(ones, value, NT, precision=HIGH, preferred_element_type=F32)
    whole = jnp.sum(inverse[0, 0:1, :])
    lam = ridge_ref[0] * (whole / K)
    for q in range(M):
        inverse[q] = 1.0 / (inverse[q] + lam)

    loop(lambda k: piece_copy(k).wait_recv())
    right = lax.fori_loop(1, n, lambda s, total: total + pieces[s], pieces[0])

    cut = (cols // 8 + 1) // 2 * 8
    streams = [(i, pl.ds(first, last - first), last - first) for i, (first, last) in enumerate([(0, cut), (cut, cols)]) if last > first]

    def copies(stream, slot):
        i, span, _ = stream
        here = swap.at[slot, book, span]
        return [
            remote(here, here, swap_send.at[slot, i, j], swap_recv.at[slot, i, j], team(dm, db))
            for j, (dm, db) in enumerate(peers)
        ]

    def send(stream, slot, value):
        swap[slot, book, stream[1]] = value
        for copy in copies(stream, slot):
            copy.start()

    def receive(stream, slot):
        for copy in copies(stream, slot):
            copy.wait()

    def apply(stream):
        _, span, size = stream
        product = None
        for q in range(M):
            left = jnp.concatenate(split2(direction[q, span]), axis=0)
            term = jnp.dot(left, halves[pl.ds(q * K, K), :], preferred_element_type=F32)
            product = term if product is None else product + term
        return (product[:size, :K] + product[size:, :K]) + (product[:size, K:] + product[size:, K:])

    def begin(stream):
        _, span, _ = stream
        receive(stream, 0)
        terms = []
        for q in range(M):
            r = swap[0, q, span]
            z = r * inverse[q, 0:1, :]
            remain[q, span] = r
            direction[q, span] = z
            solution[q, span] = jnp.zeros_like(r)
            terms.append(r * z)
        send(stream, 1, apply(stream))
        return column(terms)

    def advance(stream, slot, inner):
        _, span, _ = stream
        receive(stream, slot)
        terms = []
        for q in range(M):
            d = direction[q, span]
            terms.append(d * (swap[slot, q, span] + lam * d))
        alpha = inner / column(terms)
        terms = []
        for q in range(M):
            d = direction[q, span]
            r = remain[q, span] - alpha * (swap[slot, q, span] + lam * d)
            solution[q, span] = solution[q, span] + alpha * d
            remain[q, span] = r
            terms.append(r * (r * inverse[q, 0:1, :]))
        fresh = column(terms)
        beta = fresh / inner
        for q in range(M):
            direction[q, span] = remain[q, span] * inverse[q, 0:1, :] + beta * direction[q, span]
        return fresh

    def iterate(step, inners):
        slot = lax.rem(step, 2)
        results = []
        for stream, inner in zip(streams, inners):
            results.append(advance(stream, slot, inner))
            send(stream, 1 - slot, apply(stream))
        return tuple(results)

    for stream in streams:
        first = stream[1].start
        send(stream, 0, right[first : first + stream[2]])
    inners = lax.fori_loop(1, ITERS, iterate, tuple(begin(stream) for stream in streams))
    for stream, inner in zip(streams, inners):
        advance(stream, ITERS % 2, inner)

    span = pl.ds(blk * half, half)
    away = [
        remote(solution.at[span], books.at[mine, span], far_send.at[k], far_recv.at[k], far(k)) for k in range(1, ncg)
    ]
    for copy in away:
        copy.start()
    for q in range(M):
        books[mine, q] = solution[q]
    relays = []
    for k in range(1, ncg):
        away[k - 1].wait_recv()
        there = books.at[lax.rem(mine - k + ncg, ncg), span]
        for db in range(1, nblk):
            relay = remote(there, there, near_send.at[k, db], near_recv.at[k, db], team(0, db))
            relay.start()
            relays.append(relay)
    for relay in relays:
        relay.wait()

    for q in range(M):
        value = jnp.concatenate([books[c, q] for c in range(ncg)], axis=0)
        book_out[q] = value
        high, low = split2(value)
        parts[q, :width, :] = high
        parts[q, width:, :] = low

    size = min(256, rows)
    short = lax.broadcasted_iota(jnp.int32, (K, size), 0).astype(F32).astype(BF16)

    def rebuild(turn, total):
        at = pl.ds(pl.multiple_of(turn * size, size), size)
        value = jnp.zeros((2 * width, size), F32)
        for q in range(M):
            row = codes_ref[q : q + 1, at].astype(F32).astype(BF16)
            value = value + jnp.dot(parts[q], hot_t(row, short), preferred_element_type=F32)
        residual = vectors_ref[:, at] - (value[:width] + value[width:])
        residual_out[:, at] = residual
        return total + mass_ref[:, at] * (residual * residual)

    total = lax.fori_loop(0, rows // size, rebuild, jnp.zeros((width, size), F32))
    gathered[me] = jnp.broadcast_to(jnp.sum(total, keepdims=True), (8, 128))

    def sum_copy(k):
        return remote(gathered.at[me], gathered.at[me], sum_send.at[k], sum_recv.at[k], chip(k))

    loop(lambda k: sum_copy(k).start())
    for copy in away:
        copy.wait_send()

    def drain(k):
        codes_copy(k).wait_send()
        mass_copy(k).wait_send()
        piece_copy(k).wait_send()

    loop(drain)
    loop(lambda k: sum_copy(k).wait())
    final = lax.fori_loop(1, n, lambda s, value: value + gathered[s], gathered[0])
    sum_out[...] = final / (whole * width)


def body(vectors, codes, weights, ridge):
    rows, width = vectors.shape
    n, nblk = lax.axis_size("dp"), lax.axis_size("blk")
    gsz = M // nblk
    ncg = column_groups(n // gsz, width)
    cols = width // ncg
    shape = jax.ShapeDtypeStruct
    dma = pltpu.SemaphoreType.DMA
    state = pltpu.VMEM((M, cols, K), F32)
    books, residual, distortion = pl.pallas_call(
        functools.partial(kernel, n, nblk, ncg),
        out_shape=(shape((M, width, K), F32), shape((width, rows), F32), shape((8, 128), F32)),
        in_specs=[pl.BlockSpec(memory_space=pltpu.SMEM)] + [vmem()] * 3,
        out_specs=(vmem(),) * 3,
        scratch_shapes=[
            pltpu.VMEM((n, M, rows), jnp.int32),
            pltpu.VMEM((n, 1, rows), F32),
            pltpu.VMEM((ncg, gsz, cols, K), F32),
            pltpu.VMEM((n, cols, K), F32),
            pltpu.VMEM((M * K, K), F32),
            pltpu.VMEM((M * K, 2 * K), BF16),
            pltpu.VMEM((2, M, cols, K), F32),
            state,
            state,
            state,
            pltpu.VMEM((M, 8, K), F32),
            pltpu.VMEM((ncg, M, cols, K), F32),
            pltpu.VMEM((M, 2 * width, K), BF16),
            pltpu.VMEM((n, 8, 128), F32),
            dma((3, n)),
            dma((3, n)),
            dma((2, 2, M)),
            dma((2, 2, M)),
            dma((ncg,)),
            dma((ncg,)),
            dma((ncg, nblk)),
            dma((ncg, nblk)),
            dma((n,)),
            dma((n,)),
        ],
        compiler_params=pltpu.CompilerParams(collective_id=0, has_side_effects=True),
        name="update",
    )(ridge, codes.T, weights.astype(F32)[None, :], vectors.T)
    return (books.transpose(0, 2, 1), residual.T, distortion[0, 0])


def solution(mesh):
    return jax.shard_map(
        body,
        mesh=mesh,
        in_specs=(P("dp", None), P("dp", None), P("dp"), P()),
        out_specs=(P(), P("dp", None), P()),
        check_vma=False,
    )
```

profile of v0, /device:TPU:0, one launch (start us, length us, event | category | flops | bytes accessed | tf_op | source)
XLA Modules:
  0.0 102.7 jit_solution(14806983425982617021)
XLA Ops:
  1.3 0.0 copy-start.1
  1.3 0.7 copy-done.1
  2.0 0.6 broadcast_in_dim.7
  2.6 96.1 %update.1 = (f32[8,96,256]{2,1,0:T(8,128)}, f32[96,1024]{1,0:T(8,128)}, f32[8,128]{1,0:T(8,128)}) custom-call(f32[1]{0:T(128)S(6)} %copy.9.ridge_ref, s32[8,1024]{1,0:T(8,128)} %bitcast.9, f32[1,1024]{1,0:T(1,128)} %bitcast.10, f32[96,1024]{1,0:T(8,128)} %bitcast.8), custom_call_target="tpu_custom_call" | custom-call | tf_op jit(solution)/shard_map/update/pallas_call | solution.py:331
  98.7 1.2 %slice.3 = f32[1,1]{1,0:T(1,128)} slice(f32[8,128]{1,0:T(8,128)} %get-tuple-element.8), slice={[0:1], [0:1]} | slice | bytes 8 | tf_op jit(solution)/shard_map/slice | solution.py:365
  99.8 0.0 copy-start
  99.8 2.1 %copy.10 = f32[8,256,96]{1,2,0:T(8,128)} copy(f32[8,256,96]{1,2,0:T(8,128)} %bitcast.6) | data formatting | bytes 1572864
  102.0 0.0 copy-done
  102.0 0.7 copy.11
Async XLA Ops:
  1.3 0.7 copy-start.1
  99.8 2.1 %copy-start = (f32[96,1024]{1,0:T(8,128)S(1)}, f32[96,1024]{1,0:T(8,128)}, u32[]{:S(2)}) copy-start(f32[96,1024]{1,0:T(8,128)} %get-tuple-element.7) | copy-start | bytes 1179652
where the time goes:
time: 103 us
  Pallas kernels  96.1 us (93%)
  local copies, waits for them, and re-layouts  4.73 us (5%)
  between operations  1.3 us (1%)
    pallas_call x1, Pallas kernels, body(): pl.pallas_call(functools.partial(kernel, n, nblk, ncg), out_shape=(shape(...  96.1 us
    unnamed x6, local copies, waits for them, and re-layouts  3.54 us

commit v1 on v0

--- a/solution.py
+++ b/solution.py
@@ -180,8 +180,7 @@
     loop(lambda k: piece_copy(k).wait_recv())
     right = lax.fori_loop(1, n, lambda s, total: total + pieces[s], pieces[0])
 
-    cut = (cols // 8 + 1) // 2 * 8
-    streams = [(i, pl.ds(first, last - first), last - first) for i, (first, last) in enumerate([(0, cut), (cut, cols)]) if last > first]
+    streams = [(i, pl.ds(first, last - first), last - first) for i, (first, last) in enumerate([(c, c + 8) for c in range(0, cols, 8)])]
 
     def copies(stream, slot):
         i, span, _ = stream
@@ -350,8 +349,8 @@
             pltpu.VMEM((n, 8, 128), F32),
             dma((3, n)),
             dma((3, n)),
-            dma((2, 2, M)),
-            dma((2, 2, M)),
+            dma((2, 3, M)),
+            dma((2, 3, M)),
             dma((ncg,)),
             dma((ncg,)),
             dma((ncg, nblk)),

time: 103 us -> 98.7 us (0.958)
  Pallas kernels: 96.1 us -> 91.8 us
    pallas_call x1, Pallas kernels: 96.1 us -> 91.8 us  [body(): pl.pallas_call(functools.partial(kernel, n, nblk, ncg), out_shape=(shape(...]
where the time goes in v1:
time: 98.7 us; the launch traced here: 98.4 us
  Pallas kernels  91.8 us (93%)
  local copies, waits for them, and re-layouts  4.73 us (5%)
  between operations  1.3 us (1%)
    pallas_call x1, Pallas kernels, body(): pl.pallas_call(functools.partial(kernel, n, nblk, ncg), out_shape=(shape(...  91.8 us
    unnamed x6, local copies, waits for them, and re-layouts  3.54 us

profile of v1, /device:TPU:0, one launch (start us, length us, event | category | flops | bytes accessed | tf_op | source)
XLA Modules:
  0.0 98.4 jit_solution(12866085897472817949)
XLA Ops:
  1.3 0.0 copy-start.1
  1.3 0.7 copy-done.1
  2.0 0.6 broadcast_in_dim.7
  2.6 91.8 %update.1 = (f32[8,96,256]{2,1,0:T(8,128)}, f32[96,1024]{1,0:T(8,128)}, f32[8,128]{1,0:T(8,128)}) custom-call(f32[1]{0:T(128)S(6)} %copy.9.ridge_ref, s32[8,1024]{1,0:T(8,128)} %bitcast.9, f32[1,1024]{1,0:T(1,128)} %bitcast.10, f32[96,1024]{1,0:T(8,128)} %bitcast.8), custom_call_target="tpu_custom_call" | custom-call | tf_op jit(solution)/shard_map/update/pallas_call | solution.py:330
  94.4 1.2 %slice.3 = f32[1,1]{1,0:T(1,128)} slice(f32[8,128]{1,0:T(8,128)} %get-tuple-element.8), slice={[0:1], [0:1]} | slice | bytes 8 | tf_op jit(solution)/shard_map/slice | solution.py:364
  95.6 0.0 copy-start
  95.6 2.1 %copy.10 = f32[8,256,96]{1,2,0:T(8,128)} copy(f32[8,256,96]{1,2,0:T(8,128)} %bitcast.6) | data formatting | bytes 1572864
  97.7 0.0 copy-done
  97.7 0.7 copy.11
Async XLA Ops:
  1.3 0.7 copy-start.1
  95.6 2.1 %copy-start = (f32[96,1024]{1,0:T(8,128)S(1)}, f32[96,1024]{1,0:T(8,128)}, u32[]{:S(2)}) copy-start(f32[96,1024]{1,0:T(8,128)} %get-tuple-element.7) | copy-start | bytes 1179652

commit v2 on v1

--- a/solution.py
+++ b/solution.py
@@ -50,7 +50,7 @@
 def flip(value, mask, size):
     total, digit = 0, 1
     while digit < size:
-        total = total + digit * lax.rem(value // digit + mask // digit % 2, 2)
+        total = total + digit * lax.rem(value // digit + mask // digit, 2)
         digit *= 2
     return total
 
@@ -62,10 +62,10 @@
     return jnp.sum(total, axis=1, keepdims=True)
 
 
-def kernel(n, nblk, ncg, ridge_ref, codes_ref, mass_ref, vectors_ref, book_out, residual_out, sum_out,
-           codes_all, mass_all, part, pieces, gram, halves, swap, solution, remain, direction, inverse,
+def kernel(n, nblk, ncg, ridge_ref, codes_ref, weights_ref, vectors_ref, book_out, residual_out, sum_out,
+           mass_ref, codes_all, mass_all, part, pieces, gram, halves, swap, solution, remain, direction, inverse,
            books, parts, gathered, send_sem, recv_sem, swap_send, swap_recv, far_send, far_recv,
-           near_send, near_recv, sum_send, sum_recv):
+           near_send, near_recv, sum_send, sum_recv, pass_send, pass_recv):
     width, rows = vectors_ref.shape
     gsz = M // nblk
     cols = width // ncg
@@ -79,7 +79,7 @@
     peers = [(dm, db) for dm in range(gsz - 1, -1, -1) for db in range(nblk - 1, -1, -1) if (dm, db) != (0, 0)]
 
     def chip(k):
-        return {"dp": lax.rem(me + k, n)}
+        return {"dp": flip(me, k, n)}
 
     def team(dm, db):
         return {"dp": group * gsz + flip(member, dm, gsz), "blk": lax.rem(blk + db, nblk)}
@@ -100,6 +100,7 @@
         lax.fori_loop(1, n, step, 0)
 
     barrier = pltpu.get_barrier_semaphore()
+    mass_ref[...] = weights_ref[...].astype(F32).reshape(1, rows)
     loop(lambda k: pl.semaphore_signal(barrier, inc=1, device_id=chip(k), device_id_type=MESH))
     others = [(dm, db) for dm, db in peers if db]
     for dm, db in others:
@@ -119,14 +120,35 @@
             part[c, m] = total[c * cols : (c + 1) * cols]
     pl.semaphore_wait(barrier, n - 1 + len(others))
 
+    share = rows // nblk
+    lanes = pl.ds(pl.multiple_of(blk * share, share), share)
+
     def codes_copy(k):
-        return remote(codes_ref, codes_all.at[me], send_sem.at[0, k], recv_sem.at[0, k], chip(k))
+        source, target = codes_ref.at[:, lanes], codes_all.at[me, :, lanes]
+        return remote(source, target, send_sem.at[0, k], recv_sem.at[0, k], chip(k))
 
     def mass_copy(k):
-        return remote(mass_ref, mass_all.at[me], send_sem.at[1, k], recv_sem.at[1, k], chip(k))
+        source, target = mass_ref.at[:, lanes], mass_all.at[me, :, lanes]
+        return remote(source, target, send_sem.at[1, k], recv_sem.at[1, k], chip(k))
+
+    def passes(k):
+        there = chip(k)["dp"]
+        copies = []
+        for db in range(1, nblk):
+            for i, array in enumerate((codes_all, mass_all)):
+                piece = array.at[there, :, lanes]
+                to = {"blk": lax.rem(blk + db, nblk)}
+                copies.append(remote(piece, piece, pass_send.at[i, db, k], pass_recv.at[i, db, k], to))
+        return copies
+
+    def pass_on(k):
+        codes_copy(k).wait_recv()
+        mass_copy(k).wait_recv()
+        for copy in passes(k):
+            copy.start()
 
     def piece_copy(k):
-        to = lax.rem(me + k, n)
+        to = chip(k)["dp"]
         piece = part.at[lax.rem(to // gsz, ncg), lax.rem(to, gsz)]
         return remote(piece, pieces.at[me], send_sem.at[2, k], recv_sem.at[2, k], chip(k))
 
@@ -152,12 +174,18 @@
             gram[block(other), :] += lax.dot_general(hot, weighted, NT, preferred_element_type=F32)
 
     accumulate(me)
+    pass_on(1)
 
     def arrive(k):
-        codes_copy(k).wait_recv()
-        mass_copy(k).wait_recv()
         piece_copy(k).start()
-        accumulate(lax.rem(me - k + n, n))
+        for copy in passes(k):
+            copy.wait_recv()
+
+        @pl.when(k + 1 < n)
+        def _():
+            pass_on(k + 1)
+
+        accumulate(chip(k)["dp"])
 
     loop(arrive)
 
@@ -311,11 +339,25 @@
         codes_copy(k).wait_send()
         mass_copy(k).wait_send()
         piece_copy(k).wait_send()
+        for copy in passes(k):
+            copy.wait_send()
 
     loop(drain)
     loop(lambda k: sum_copy(k).wait())
     final = lax.fori_loop(1, n, lambda s, value: value + gathered[s], gathered[0])
     sum_out[...] = final / (whole * width)
+
+
+def store(books_ref, residual_ref, sum_ref, books_out, residual_out, sum_out, sems):
+    copies = [
+        pltpu.make_async_copy(books_ref, books_out, sems.at[0]),
+        pltpu.make_async_copy(residual_ref, residual_out, sems.at[1]),
+    ]
+    for copy in copies:
+        copy.start()
+    sum_out[...] = sum_ref[0:1, 0:1]
+    for copy in copies:
+        copy.wait()
 
 
 def body(vectors, codes, weights, ridge):
@@ -329,10 +371,11 @@
     state = pltpu.VMEM((M, cols, K), F32)
     books, residual, distortion = pl.pallas_call(
         functools.partial(kernel, n, nblk, ncg),
-        out_shape=(shape((M, width, K), F32), shape((width, rows), F32), shape((8, 128), F32)),
+        out_shape=(pltpu.VMEM((M, width, K), F32), pltpu.VMEM((width, rows), F32), pltpu.VMEM((8, 128), F32)),
         in_specs=[pl.BlockSpec(memory_space=pltpu.SMEM)] + [vmem()] * 3,
         out_specs=(vmem(),) * 3,
         scratch_shapes=[
+            pltpu.VMEM((1, rows), F32),
             pltpu.VMEM((n, M, rows), jnp.int32),
             pltpu.VMEM((n, 1, rows), F32),
             pltpu.VMEM((ncg, gsz, cols, K), F32),
@@ -357,10 +400,20 @@
             dma((ncg, nblk)),
             dma((n,)),
             dma((n,)),
+            dma((2, nblk, n)),
+            dma((2, nblk, n)),
         ],
         compiler_params=pltpu.CompilerParams(collective_id=0, has_side_effects=True),
         name="update",
-    )(ridge, codes.T, weights.astype(F32)[None, :], vectors.T)
+    )(ridge, codes.T, weights, vectors.T)
+    books, residual, distortion = pl.pallas_call(
+        store,
+        out_shape=(shape((M, width, K), F32), shape((width, rows), F32), shape((1, 1), F32)),
+        in_specs=[vmem()] * 3,
+        out_specs=(pl.BlockSpec(memory_space=pl.ANY), pl.BlockSpec(memory_space=pl.ANY), vmem()),
+        scratch_shapes=[dma((2,))],
+        name="store",
+    )(*(pltpu.with_memory_space_constraint(value, pltpu.VMEM) for value in (books, residual, distortion)))
     return (books.transpose(0, 2, 1), residual.T, distortion[0, 0])
 
 

time: 98.7 us -> 93.4 us (0.946)
  local copies, waits for them, and re-layouts: 4.73 us -> 0 us
    unnamed x6 -> x0, local copies, waits for them, and re-layouts: 3.54 us -> none
    slice x1 -> x0, local copies, waits for them, and re-layouts: 1.19 us -> none  [body(): return (books.transpose(0, 2, 1), residual.T, distortion[0, 0])]
    pallas_call x1 -> x2, Pallas kernels: 91.8 us -> 92 us  [the longest x1 90.5 us: body(): pl.pallas_call(functools.partial(kernel, n, nblk, ncg), out_shape=(pltpu....]
where the time goes in v2:
time: 93.4 us; the launch traced here: 93.3 us
  Pallas kernels  92 us (99%)
  between operations  1.29 us (1%)
    pallas_call x1, Pallas kernels, body(): pl.pallas_call(functools.partial(kernel, n, nblk, ncg), out_shape=(pltpu....  90.5 us

profile of v2, /device:TPU:0, one launch (start us, length us, event | category | flops | bytes accessed | tf_op | source)
XLA Modules:
  0.0 93.3 jit_solution(7146966178664452900)
XLA Ops:
  1.3 90.5 %update.1 = (f32[8,96,256]{2,1,0:T(8,128)S(1)}, f32[96,1024]{1,0:T(8,128)S(1)}, f32[8,128]{1,0:T(8,128)S(1)}) custom-call(f32[1]{0:T(128)S(6)} %copy.7.ridge_ref, s32[8,1024]{1,0:T(8,128)} %bitcast.6, bf16[1024]{0:T(1024)(128)(2,1)} %weights_ref.1, f32[96,1024]{1,0:T(8,128)} %bitcast.5), custom_call_target="tpu_custom_call" | custom-call | tf_op jit(solution)/shard_map/update/pallas_call | solution.py:372
  91.8 1.5 %store.1 = (f32[8,96,256]{2,1,0:T(8,128)}, f32[96,1024]{1,0:T(8,128)}, f32[1,1]{1,0:T(1,128)}) custom-call(f32[8,96,256]{2,1,0:T(8,128)S(1)} %get-tuple-element.9.books_ref, f32[96,1024]{1,0:T(8,128)S(1)} %get-tuple-element.10.residual_ref, f32[8,128]{1,0:T(8,128)S(1)} %get-tuple-element.11.sum_ref), custom_call_target="tpu_custom_call" | custom-call | tf_op jit(solution)/shard_map/store/pallas_call | solution.py:409

commit v3 on v2

--- a/solution.py
+++ b/solution.py
@@ -65,7 +65,8 @@
 def kernel(n, nblk, ncg, ridge_ref, codes_ref, weights_ref, vectors_ref, book_out, residual_out, sum_out,
            mass_ref, codes_all, mass_all, part, pieces, gram, halves, swap, solution, remain, direction, inverse,
            books, parts, gathered, send_sem, recv_sem, swap_send, swap_recv, far_send, far_recv,
-           near_send, near_recv, sum_send, sum_recv, pass_send, pass_recv):
+           near_send, near_recv, sum_send, sum_recv, pass_send, pass_recv, crew, team_parts, pairs,
+           team_send, team_recv, pair_send, pair_recv):
     width, rows = vectors_ref.shape
     gsz = M // nblk
     cols = width // ncg
@@ -208,6 +209,17 @@
     loop(lambda k: piece_copy(k).wait_recv())
     right = lax.fori_loop(1, n, lambda s, total: total + pieces[s], pieces[0])
 
+    def band(c):
+        return pl.ds(pl.multiple_of(c * cols, 8), cols)
+
+    def team_copy(k):
+        source, target = vectors_ref.at[band(lax.rem(mine + k, ncg)), lanes], crew.at[mine]
+        return remote(source, target, team_send.at[k], team_recv.at[k], far(k))
+
+    for k in range(1, ncg):
+        team_copy(k).start()
+    crew[mine] = vectors_ref[band(mine), lanes]
+
     streams = [(i, pl.ds(first, last - first), last - first) for i, (first, last) in enumerate([(c, c + 8) for c in range(0, cols, 8)])]
 
     def copies(stream, slot):
@@ -283,25 +295,70 @@
         first = stream[1].start
         send(stream, 0, right[first : first + stream[2]])
     inners = lax.fori_loop(1, ITERS, iterate, tuple(begin(stream) for stream in streams))
+    span = pl.ds(blk * half, half)
+
+    def away(stream, k):
+        i, place, _ = stream
+        source, target = solution.at[span, place], books.at[mine, span, place]
+        return remote(source, target, far_send.at[i, k], far_recv.at[i, k], far(k))
+
     for stream, inner in zip(streams, inners):
         advance(stream, ITERS % 2, inner)
-
-    span = pl.ds(blk * half, half)
-    away = [
-        remote(solution.at[span], books.at[mine, span], far_send.at[k], far_recv.at[k], far(k)) for k in range(1, ncg)
+        for k in range(1, ncg):
+            away(stream, k).start()
+
+    for q in range(M):
+        value = solution[q]
+        books[mine, q] = value
+        high = value.astype(BF16).astype(F32)
+        team_parts[q] = jnp.concatenate([high, value - high], axis=0).astype(BF16)
+    for k in range(1, ncg):
+        team_copy(k).wait()
+    size = min(256, share)
+    short = lax.broadcasted_iota(jnp.int32, (K, size), 0).astype(F32).astype(BF16)
+
+    def squares(turn, total):
+        c, first = lax.div(turn, share // size), lax.rem(turn, share // size) * size
+        source = (bases + c) * gsz + member
+        at = pl.ds(pl.multiple_of(blk * share + first, size), size)
+        value = jnp.zeros((2 * cols, size), F32)
+        for q in range(M):
+            row = codes_all[source, q : q + 1, at].astype(F32).astype(BF16)
+            value = value + jnp.dot(team_parts[q], hot_t(row, short), preferred_element_type=F32)
+        residual = crew[c, :, pl.ds(pl.multiple_of(first, size), size)] - (value[:cols] + value[cols:])
+        return total + mass_all[source, :, at] * (residual * residual)
+
+    total = lax.fori_loop(0, ncg * (share // size), squares, jnp.zeros((cols, size), F32))
+    pairs[blk] = jnp.broadcast_to(jnp.sum(total, keepdims=True), (8, 128))
+    beside = [
+        remote(pairs.at[blk], pairs.at[blk], pair_send.at[db], pair_recv.at[db], {"blk": lax.rem(blk + db, nblk)})
+        for db in range(1, nblk)
     ]
-    for copy in away:
+    for copy in beside:
         copy.start()
-    for q in range(M):
-        books[mine, q] = solution[q]
+    for copy in beside:
+        copy.wait()
+    both = pairs[0]
+    for b in range(1, nblk):
+        both = both + pairs[b]
+    gathered[me] = both
+
+    def sum_copy(k):
+        row = gathered.at[me, pl.ds(0, 1)]
+        return remote(row, row, sum_send.at[k], sum_recv.at[k], chip(k))
+
+    loop(lambda k: sum_copy(k).start())
+
     relays = []
-    for k in range(1, ncg):
-        away[k - 1].wait_recv()
-        there = books.at[lax.rem(mine - k + ncg, ncg), span]
-        for db in range(1, nblk):
-            relay = remote(there, there, near_send.at[k, db], near_recv.at[k, db], team(0, db))
-            relay.start()
-            relays.append(relay)
+    for stream in streams:
+        i, place, _ = stream
+        for k in range(1, ncg):
+            away(stream, k).wait_recv()
+            there = books.at[lax.rem(mine - k + ncg, ncg), span, place]
+            for db in range(1, nblk):
+                relay = remote(there, there, near_send.at[i, k, db], near_recv.at[i, k, db], team(0, db))
+                relay.start()
+                relays.append(relay)
     for relay in relays:
         relay.wait()
 
@@ -312,28 +369,18 @@
         parts[q, :width, :] = high
         parts[q, width:, :] = low
 
-    size = min(256, rows)
-    short = lax.broadcasted_iota(jnp.int32, (K, size), 0).astype(F32).astype(BF16)
-
-    def rebuild(turn, total):
+    def rebuild(turn):
         at = pl.ds(pl.multiple_of(turn * size, size), size)
         value = jnp.zeros((2 * width, size), F32)
         for q in range(M):
             row = codes_ref[q : q + 1, at].astype(F32).astype(BF16)
             value = value + jnp.dot(parts[q], hot_t(row, short), preferred_element_type=F32)
-        residual = vectors_ref[:, at] - (value[:width] + value[width:])
-        residual_out[:, at] = residual
-        return total + mass_ref[:, at] * (residual * residual)
-
-    total = lax.fori_loop(0, rows // size, rebuild, jnp.zeros((width, size), F32))
-    gathered[me] = jnp.broadcast_to(jnp.sum(total, keepdims=True), (8, 128))
-
-    def sum_copy(k):
-        return remote(gathered.at[me], gathered.at[me], sum_send.at[k], sum_recv.at[k], chip(k))
-
-    loop(lambda k: sum_copy(k).start())
-    for copy in away:
-        copy.wait_send()
+        residual_out[:, at] = vectors_ref[:, at] - (value[:width] + value[width:])
+
+    pl.loop(0, rows // size)(rebuild)
+    for stream in streams:
+        for k in range(1, ncg):
+            away(stream, k).wait_send()
 
     def drain(k):
         codes_copy(k).wait_send()
@@ -344,8 +391,8 @@
 
     loop(drain)
     loop(lambda k: sum_copy(k).wait())
-    final = lax.fori_loop(1, n, lambda s, value: value + gathered[s], gathered[0])
-    sum_out[...] = final / (whole * width)
+    final = lax.fori_loop(1, n, lambda s, value: value + gathered[s, 0:1], gathered[0, 0:1])
+    sum_out[...] = jnp.broadcast_to(final / (whole * width), (8, 128))
 
 
 def store(books_ref, residual_ref, sum_ref, books_out, residual_out, sum_out, sems):
@@ -394,14 +441,21 @@
             dma((3, n)),
             dma((2, 3, M)),
             dma((2, 3, M)),
-            dma((ncg,)),
-            dma((ncg,)),
-            dma((ncg, nblk)),
-            dma((ncg, nblk)),
+            dma((cols // 8, ncg)),
+            dma((cols // 8, ncg)),
+            dma((cols // 8, ncg, nblk)),
+            dma((cols // 8, ncg, nblk)),
             dma((n,)),
             dma((n,)),
             dma((2, nblk, n)),
             dma((2, nblk, n)),
+            pltpu.VMEM((ncg, cols, rows // nblk), F32),
+            pltpu.VMEM((M, 2 * cols, K), BF16),
+            pltpu.VMEM((nblk, 8, 128), F32),
+            dma((ncg,)),
+            dma((ncg,)),
+            dma((nblk,)),
+            dma((nblk,)),
         ],
         compiler_params=pltpu.CompilerParams(collective_id=0, has_side_effects=True),
         name="update",

time: 93.4 us -> 87.9 us (0.941)
  Pallas kernels: 92 us -> 86.5 us
    pallas_call x1, Pallas kernels: 90.5 us -> 85 us  [body(): pl.pallas_call(functools.partial(kernel, n, nblk, ncg), out_shape=(pltpu....]
where the time goes in v3:
time: 87.9 us; the launch traced here: 87.8 us
  Pallas kernels  86.5 us (98%)
  between operations  1.29 us (1%)
    pallas_call x1, Pallas kernels, body(): pl.pallas_call(functools.partial(kernel, n, nblk, ncg), out_shape=(pltpu....  85 us

profile of v3, /device:TPU:0, one launch (start us, length us, event | category | flops | bytes accessed | tf_op | source)
XLA Modules:
  0.0 87.8 jit_solution(6116982985401952203)
XLA Ops:
  1.3 85.0 %update.1 = (f32[8,96,256]{2,1,0:T(8,128)S(1)}, f32[96,1024]{1,0:T(8,128)S(1)}, f32[8,128]{1,0:T(8,128)S(1)}) custom-call(f32[1]{0:T(128)S(6)} %copy.7.ridge_ref, s32[8,1024]{1,0:T(8,128)} %bitcast.6, bf16[1024]{0:T(1024)(128)(2,1)} %weights_ref.1, f32[96,1024]{1,0:T(8,128)} %bitcast.5), custom_call_target="tpu_custom_call" | custom-call | tf_op jit(solution)/shard_map/update/pallas_call | solution.py:419
  86.2 1.5 %store.1 = (f32[8,96,256]{2,1,0:T(8,128)}, f32[96,1024]{1,0:T(8,128)}, f32[1,1]{1,0:T(1,128)}) custom-call(f32[8,96,256]{2,1,0:T(8,128)S(1)} %get-tuple-element.9.books_ref, f32[96,1024]{1,0:T(8,128)S(1)} %get-tuple-element.10.residual_ref, f32[8,128]{1,0:T(8,128)S(1)} %get-tuple-element.11.sum_ref), custom_call_target="tpu_custom_call" | custom-call | tf_op jit(solution)/shard_map/store/pallas_call | solution.py:463

commit v4 on v3

--- a/solution.py
+++ b/solution.py
@@ -10,6 +10,7 @@
 K = 256
 M = 8
 ITERS = 8
+LATE = 3
 MESH = pl.DeviceIdType.MESH
 HIGH = lax.Precision.HIGHEST
 F32 = jnp.float32
@@ -65,7 +66,7 @@
 def kernel(n, nblk, ncg, ridge_ref, codes_ref, weights_ref, vectors_ref, book_out, residual_out, sum_out,
            mass_ref, codes_all, mass_all, part, pieces, gram, halves, swap, solution, remain, direction, inverse,
            books, parts, gathered, send_sem, recv_sem, swap_send, swap_recv, far_send, far_recv,
-           near_send, near_recv, sum_send, sum_recv, pass_send, pass_recv, crew, team_parts, pairs,
+           near_send, near_recv, sum_send, sum_recv, pass_send, pass_recv, counts, crew, team_parts, pairs,
            team_send, team_recv, pair_send, pair_recv):
     width, rows = vectors_ref.shape
     gsz = M // nblk
@@ -158,6 +159,7 @@
         mass_copy(k).start()
 
     loop(send_codes)
+    loop(lambda k: piece_copy(k).start())
 
     codes_all[me] = codes_ref[...]
     mass_all[me] = mass_ref[...]
@@ -176,49 +178,6 @@
 
     accumulate(me)
     pass_on(1)
-
-    def arrive(k):
-        piece_copy(k).start()
-        for copy in passes(k):
-            copy.wait_recv()
-
-        @pl.when(k + 1 < n)
-        def _():
-            pass_on(k + 1)
-
-        accumulate(chip(k)["dp"])
-
-    loop(arrive)
-
-    square = (K, K)
-    own = jnp.sum(gram[block(lax.rem(book + 1, M)), :], axis=0, keepdims=True)
-    diagonal = lax.broadcasted_iota(jnp.int32, square, 0) == lax.broadcasted_iota(jnp.int32, square, 1)
-    gram[block(book), :] = jnp.where(diagonal, jnp.broadcast_to(own, square), 0.0)
-    ones = jnp.ones((8, K), F32)
-    for q in range(M):
-        value = gram[block(q), :]
-        high, low = split2(value)
-        halves[block(q), :K] = high
-        halves[block(q), K:] = low
-        inverse[q] = lax.dot_general(ones, value, NT, precision=HIGH, preferred_element_type=F32)
-    whole = jnp.sum(inverse[0, 0:1, :])
-    lam = ridge_ref[0] * (whole / K)
-    for q in range(M):
-        inverse[q] = 1.0 / (inverse[q] + lam)
-
-    loop(lambda k: piece_copy(k).wait_recv())
-    right = lax.fori_loop(1, n, lambda s, total: total + pieces[s], pieces[0])
-
-    def band(c):
-        return pl.ds(pl.multiple_of(c * cols, 8), cols)
-
-    def team_copy(k):
-        source, target = vectors_ref.at[band(lax.rem(mine + k, ncg)), lanes], crew.at[mine]
-        return remote(source, target, team_send.at[k], team_recv.at[k], far(k))
-
-    for k in range(1, ncg):
-        team_copy(k).start()
-    crew[mine] = vectors_ref[band(mine), lanes]
 
     streams = [(i, pl.ds(first, last - first), last - first) for i, (first, last) in enumerate([(c, c + 8) for c in range(0, cols, 8)])]
 
@@ -235,6 +194,56 @@
         for copy in copies(stream, slot):
             copy.start()
 
+    def open_streams():
+        loop(lambda k: piece_copy(k).wait_recv())
+        right = lax.fori_loop(1, n, lambda s, total: total + pieces[s], pieces[0])
+        for stream in streams:
+            first = stream[1].start
+            send(stream, 0, right[first : first + stream[2]])
+
+    def arrive(k):
+        pl.when(k == max(n - LATE, 1))(open_streams)
+        for copy in passes(k):
+            copy.wait_recv()
+
+        @pl.when(k + 1 < n)
+        def _():
+            pass_on(k + 1)
+
+        accumulate(chip(k)["dp"])
+
+    loop(arrive)
+
+    own = jnp.sum(gram[block(lax.rem(book + 1, M)), :], axis=0, keepdims=True)
+    inverse[book] = jnp.broadcast_to(own, (8, K))
+    counts[...] = inverse[book]
+    ones = jnp.ones((8, K), BF16)
+    for j in range(1, M):
+        other = lax.rem(book + j, M)
+        high, low, rest = split3(gram[block(other), :])
+        halves[block(other), :K] = high
+        halves[block(other), K:] = low
+        total = None
+        for piece in (high, low, rest):
+            term = lax.dot_general(ones, piece, NT, preferred_element_type=F32)
+            total = term if total is None else total + term
+        inverse[other] = total
+    whole = jnp.sum(inverse[0, 0:1, :])
+    lam = ridge_ref[0] * (whole / K)
+    for q in range(M):
+        inverse[q] = 1.0 / (inverse[q] + lam)
+
+    def band(c):
+        return pl.ds(pl.multiple_of(c * cols, 8), cols)
+
+    def team_copy(k):
+        source, target = vectors_ref.at[band(lax.rem(mine + k, ncg)), lanes], crew.at[mine]
+        return remote(source, target, team_send.at[k], team_recv.at[k], far(k))
+
+    for k in range(1, ncg):
+        team_copy(k).start()
+    crew[mine] = vectors_ref[band(mine), lanes]
+
     def receive(stream, slot):
         for copy in copies(stream, slot):
             copy.wait()
@@ -242,11 +251,13 @@
     def apply(stream):
         _, span, size = stream
         product = None
-        for q in range(M):
-            left = jnp.concatenate(split2(direction[q, span]), axis=0)
-            term = jnp.dot(left, halves[pl.ds(q * K, K), :], preferred_element_type=F32)
+        for j in range(1, M):
+            other = lax.rem(book + j, M)
+            left = jnp.concatenate(split2(direction[other, span]), axis=0)
+            term = jnp.dot(left, halves[block(other), :], preferred_element_type=F32)
             product = term if product is None else product + term
-        return (product[:size, :K] + product[size:, :K]) + (product[:size, K:] + product[size:, K:])
+        total = (product[:size, :K] + product[size:, :K]) + (product[:size, K:] + product[size:, K:])
+        return total + counts[0:1, :] * direction[book, span]
 
     def begin(stream):
         _, span, _ = stream
@@ -291,9 +302,6 @@
             send(stream, 1 - slot, apply(stream))
         return tuple(results)
 
-    for stream in streams:
-        first = stream[1].start
-        send(stream, 0, right[first : first + stream[2]])
     inners = lax.fori_loop(1, ITERS, iterate, tuple(begin(stream) for stream in streams))
     span = pl.ds(blk * half, half)
 
@@ -449,6 +457,7 @@
             dma((n,)),
             dma((2, nblk, n)),
             dma((2, nblk, n)),
+            pltpu.VMEM((8, K), F32),
             pltpu.VMEM((ncg, cols, rows // nblk), F32),
             pltpu.VMEM((M, 2 * cols, K), BF16),
             pltpu.VMEM((nblk, 8, 128), F32),

time: 87.9 us -> 82.6 us (0.940)
  Pallas kernels: 86.5 us -> 81.2 us
    pallas_call x1, Pallas kernels: 85 us -> 79.6 us  [body(): pl.pallas_call(functools.partial(kernel, n, nblk, ncg), out_shape=(pltpu....]
where the time goes in v4:
time: 82.6 us; the launch traced here: 82.5 us
  Pallas kernels  81.2 us (98%)
  between operations  1.29 us (2%)
    pallas_call x1, Pallas kernels, body(): pl.pallas_call(functools.partial(kernel, n, nblk, ncg), out_shape=(pltpu....  79.6 us

profile of v4, /device:TPU:0, one launch (start us, length us, event | category | flops | bytes accessed | tf_op | source)
XLA Modules:
  0.0 82.5 jit_solution(7375304497126965201)
XLA Ops:
  1.3 79.6 %update.1 = (f32[8,96,256]{2,1,0:T(8,128)S(1)}, f32[96,1024]{1,0:T(8,128)S(1)}, f32[8,128]{1,0:T(8,128)S(1)}) custom-call(f32[1]{0:T(128)S(6)} %copy.7.ridge_ref, s32[8,1024]{1,0:T(8,128)} %bitcast.6, bf16[1024]{0:T(1024)(128)(2,1)} %weights_ref.1, f32[96,1024]{1,0:T(8,128)} %bitcast.5), custom_call_target="tpu_custom_call" | custom-call | tf_op jit(solution)/shard_map/update/pallas_call | solution.py:427
  80.9 1.5 %store.1 = (f32[8,96,256]{2,1,0:T(8,128)}, f32[96,1024]{1,0:T(8,128)}, f32[1,1]{1,0:T(1,128)}) custom-call(f32[8,96,256]{2,1,0:T(8,128)S(1)} %get-tuple-element.9.books_ref, f32[96,1024]{1,0:T(8,128)S(1)} %get-tuple-element.10.residual_ref, f32[8,128]{1,0:T(8,128)S(1)} %get-tuple-element.11.sum_ref), custom_call_target="tpu_custom_call" | custom-call | tf_op jit(solution)/shard_map/store/pallas_call | solution.py:472

commit v5 on v4

--- a/solution.py
+++ b/solution.py
@@ -63,12 +63,12 @@
     return jnp.sum(total, axis=1, keepdims=True)
 
 
-def kernel(n, nblk, ncg, ridge_ref, codes_ref, weights_ref, vectors_ref, book_out, residual_out, sum_out,
-           mass_ref, codes_all, mass_all, part, pieces, gram, halves, swap, solution, remain, direction, inverse,
+def kernel(n, nblk, ncg, ridge_ref, codes_in, weights_ref, vectors_in, book_out, residual_out, sum_out,
+           codes_ref, vectors_ref, load_sem, mass_ref, codes_all, mass_all, part, pieces, gram, halves, swap, solution, remain, direction, inverse,
            books, parts, gathered, send_sem, recv_sem, swap_send, swap_recv, far_send, far_recv,
            near_send, near_recv, sum_send, sum_recv, pass_send, pass_recv, counts, crew, team_parts, pairs,
            team_send, team_recv, pair_send, pair_recv):
-    width, rows = vectors_ref.shape
+    width, rows = vectors_in.shape
     gsz = M // nblk
     cols = width // ncg
     me = lax.axis_index("dp")
@@ -108,6 +108,14 @@
     for dm, db in others:
         pl.semaphore_signal(barrier, inc=1, device_id=team(dm, db), device_id_type=MESH)
 
+    loads = [
+        pltpu.make_async_copy(codes_in, codes_ref, load_sem.at[0]),
+        pltpu.make_async_copy(vectors_in, vectors_ref, load_sem.at[1]),
+    ]
+    for copy in loads:
+        copy.start()
+    for copy in loads:
+        copy.wait()
     triple = jnp.concatenate(split3(vectors_ref[...]), axis=0)
     levels = lax.broadcasted_iota(jnp.int32, (K, rows), 0).astype(F32).astype(BF16)
 
@@ -221,8 +229,8 @@
     for j in range(1, M):
         other = lax.rem(book + j, M)
         high, low, rest = split3(gram[block(other), :])
-        halves[block(other), :K] = high
-        halves[block(other), K:] = low
+        halves[(j - 1) * K : j * K, :K] = high
+        halves[(j - 1) * K : j * K, K:] = low
         total = None
         for piece in (high, low, rest):
             term = lax.dot_general(ones, piece, NT, preferred_element_type=F32)
@@ -250,12 +258,10 @@
 
     def apply(stream):
         _, span, size = stream
-        product = None
+        lefts = []
         for j in range(1, M):
-            other = lax.rem(book + j, M)
-            left = jnp.concatenate(split2(direction[other, span]), axis=0)
-            term = jnp.dot(left, halves[block(other), :], preferred_element_type=F32)
-            product = term if product is None else product + term
+            lefts.append(jnp.concatenate(split2(direction[lax.rem(book + j, M), span]), axis=0))
+        product = jnp.dot(jnp.concatenate(lefts, axis=1), halves[...], preferred_element_type=F32)
         total = (product[:size, :K] + product[size:, :K]) + (product[:size, K:] + product[size:, K:])
         return total + counts[0:1, :] * direction[book, span]
 
@@ -294,6 +300,17 @@
             direction[q, span] = remain[q, span] * inverse[q, 0:1, :] + beta * direction[q, span]
         return fresh
 
+    def finish(stream, slot, inner):
+        _, span, _ = stream
+        receive(stream, slot)
+        terms = []
+        for q in range(M):
+            d = direction[q, span]
+            terms.append(d * (swap[slot, q, span] + lam * d))
+        alpha = inner / column(terms)
+        for q in range(M):
+            books[mine, q, span] = solution[q, span] + alpha * direction[q, span]
+
     def iterate(step, inners):
         slot = lax.rem(step, 2)
         results = []
@@ -307,17 +324,16 @@
 
     def away(stream, k):
         i, place, _ = stream
-        source, target = solution.at[span, place], books.at[mine, span, place]
-        return remote(source, target, far_send.at[i, k], far_recv.at[i, k], far(k))
+        piece = books.at[mine, span, place]
+        return remote(piece, piece, far_send.at[i, k], far_recv.at[i, k], far(k))
 
     for stream, inner in zip(streams, inners):
-        advance(stream, ITERS % 2, inner)
+        finish(stream, ITERS % 2, inner)
         for k in range(1, ncg):
             away(stream, k).start()
 
     for q in range(M):
-        value = solution[q]
-        books[mine, q] = value
+        value = books[mine, q]
         high = value.astype(BF16).astype(F32)
         team_parts[q] = jnp.concatenate([high, value - high], axis=0).astype(BF16)
     for k in range(1, ncg):
@@ -427,16 +443,19 @@
     books, residual, distortion = pl.pallas_call(
         functools.partial(kernel, n, nblk, ncg),
         out_shape=(pltpu.VMEM((M, width, K), F32), pltpu.VMEM((width, rows), F32), pltpu.VMEM((8, 128), F32)),
-        in_specs=[pl.BlockSpec(memory_space=pltpu.SMEM)] + [vmem()] * 3,
+        in_specs=[pl.BlockSpec(memory_space=pltpu.SMEM), pl.BlockSpec(memory_space=pl.ANY), vmem(), pl.BlockSpec(memory_space=pl.ANY)],
         out_specs=(vmem(),) * 3,
         scratch_shapes=[
+            pltpu.VMEM((M, rows), jnp.int32),
+            pltpu.VMEM((width, rows), F32),
+            dma((2,)),
             pltpu.VMEM((1, rows), F32),
             pltpu.VMEM((n, M, rows), jnp.int32),
             pltpu.VMEM((n, 1, rows), F32),
             pltpu.VMEM((ncg, gsz, cols, K), F32),
             pltpu.VMEM((n, cols, K), F32),
             pltpu.VMEM((M * K, K), F32),
-            pltpu.VMEM((M * K, 2 * K), BF16),
+            pltpu.VMEM(((M - 1) * K, 2 * K), BF16),
             pltpu.VMEM((2, M, cols, K), F32),
             state,
             state,

time: 82.6 us -> 82 us (level)
  no operation moved by 1% of the time
where the time goes in v5:
time: 82 us; the launch traced here: 81.8 us
  Pallas kernels  80.6 us (98%)
  between operations  1.29 us (2%)
    pallas_call x1, Pallas kernels, body(): pl.pallas_call(functools.partial(kernel, n, nblk, ncg), out_shape=(pltpu....  79 us

profile of v5, /device:TPU:0, one launch (start us, length us, event | category | flops | bytes accessed | tf_op | source)
XLA Modules:
  0.0 81.8 jit_solution(12005177735653739820)
XLA Ops:
  1.3 79.0 %update.1 = (f32[8,96,256]{2,1,0:T(8,128)S(1)}, f32[96,1024]{1,0:T(8,128)S(1)}, f32[8,128]{1,0:T(8,128)S(1)}) custom-call(f32[1]{0:T(128)S(6)} %copy.7.ridge_ref, s32[8,1024]{1,0:T(8,128)} %bitcast.6, bf16[1024]{0:T(1024)(128)(2,1)} %weights_ref.1, f32[96,1024]{1,0:T(8,128)} %bitcast.5), custom_call_target="tpu_custom_call" | custom-call | tf_op jit(solution)/shard_map/update/pallas_call | solution.py:443
  80.3 1.5 %store.1 = (f32[8,96,256]{2,1,0:T(8,128)}, f32[96,1024]{1,0:T(8,128)}, f32[1,1]{1,0:T(1,128)}) custom-call(f32[8,96,256]{2,1,0:T(8,128)S(1)} %get-tuple-element.9.books_ref, f32[96,1024]{1,0:T(8,128)S(1)} %get-tuple-element.10.residual_ref, f32[8,128]{1,0:T(8,128)S(1)} %get-tuple-element.11.sum_ref), custom_call_target="tpu_custom_call" | custom-call | tf_op jit(solution)/shard_map/store/pallas_call | solution.py:491

commit v6 on v5

--- a/solution.py
+++ b/solution.py
@@ -189,17 +189,17 @@
 
     streams = [(i, pl.ds(first, last - first), last - first) for i, (first, last) in enumerate([(c, c + 8) for c in range(0, cols, 8)])]
 
-    def copies(stream, slot):
+    def copies(stream, slot, short_form=False):
         i, span, _ = stream
-        here = swap.at[slot, book, span]
+        here = swap.at[slot, book, span] if not short_form else swap.at[slot, book, span, pl.ds(0, K // 2)]
         return [
             remote(here, here, swap_send.at[slot, i, j], swap_recv.at[slot, i, j], team(dm, db))
             for j, (dm, db) in enumerate(peers)
         ]
 
-    def send(stream, slot, value):
-        swap[slot, book, stream[1]] = value
-        for copy in copies(stream, slot):
+    def send(stream, slot, value, short_form=False):
+        swap[slot, book, stream[1], : value.shape[1]] = value
+        for copy in copies(stream, slot, short_form):
             copy.start()
 
     def open_streams():
@@ -252,8 +252,8 @@
         team_copy(k).start()
     crew[mine] = vectors_ref[band(mine), lanes]
 
-    def receive(stream, slot):
-        for copy in copies(stream, slot):
+    def receive(stream, slot, short_form=False):
+        for copy in copies(stream, slot, short_form):
             copy.wait()
 
     def apply(stream):
@@ -302,12 +302,8 @@
 
     def finish(stream, slot, inner):
         _, span, _ = stream
-        receive(stream, slot)
-        terms = []
-        for q in range(M):
-            d = direction[q, span]
-            terms.append(d * (swap[slot, q, span] + lam * d))
-        alpha = inner / column(terms)
+        receive(stream, slot, True)
+        alpha = inner / column([swap[slot, q, span, : K // 2] for q in range(M)])
         for q in range(M):
             books[mine, q, span] = solution[q, span] + alpha * direction[q, span]
 
@@ -319,7 +315,18 @@
             send(stream, 1 - slot, apply(stream))
         return tuple(results)
 
-    inners = lax.fori_loop(1, ITERS, iterate, tuple(begin(stream) for stream in streams))
+    def last(step, inners):
+        slot = step % 2
+        results = []
+        for stream, inner in zip(streams, inners):
+            results.append(advance(stream, slot, inner))
+            d = direction[book, stream[1]]
+            part = d * (apply(stream) + lam * d)
+            send(stream, 1 - slot, part[:, : K // 2] + part[:, K // 2 :], True)
+        return tuple(results)
+
+    inners = lax.fori_loop(1, ITERS - 1, iterate, tuple(begin(stream) for stream in streams))
+    inners = last(ITERS - 1, inners)
     span = pl.ds(blk * half, half)
 
     def away(stream, k):
@@ -390,15 +397,13 @@
         value = jnp.concatenate([books[c, q] for c in range(ncg)], axis=0)
         book_out[q] = value
         high, low = split2(value)
-        parts[q, :width, :] = high
-        parts[q, width:, :] = low
+        parts[:width, q * K : (q + 1) * K] = high
+        parts[width:, q * K : (q + 1) * K] = low
 
     def rebuild(turn):
         at = pl.ds(pl.multiple_of(turn * size, size), size)
-        value = jnp.zeros((2 * width, size), F32)
-        for q in range(M):
-            row = codes_ref[q : q + 1, at].astype(F32).astype(BF16)
-            value = value + jnp.dot(parts[q], hot_t(row, short), preferred_element_type=F32)
+        hots = [hot_t(codes_ref[q : q + 1, at].astype(F32).astype(BF16), short) for q in range(M)]
+        value = jnp.dot(parts[...], jnp.concatenate(hots, axis=0), preferred_element_type=F32)
         residual_out[:, at] = vectors_ref[:, at] - (value[:width] + value[width:])
 
     pl.loop(0, rows // size)(rebuild)
@@ -462,7 +467,7 @@
             state,
             pltpu.VMEM((M, 8, K), F32),
             pltpu.VMEM((ncg, M, cols, K), F32),
-            pltpu.VMEM((M, 2 * width, K), BF16),
+            pltpu.VMEM((2 * width, M * K), BF16),
             pltpu.VMEM((n, 8, 128), F32),
             dma((3, n)),
             dma((3, n)),

time: 82 us -> 81.9 us (level)
  no operation moved by 1% of the time
where the time goes in v6:
time: 81.9 us; the launch traced here: 81.7 us
  Pallas kernels  80.4 us (98%)
  between operations  1.29 us (2%)
    pallas_call x1, Pallas kernels, body(): pl.pallas_call(functools.partial(kernel, n, nblk, ncg), out_shape=(pltpu....  78.9 us

profile of v6, /device:TPU:0, one launch (start us, length us, event | category | flops | bytes accessed | tf_op | source)
XLA Modules:
  0.0 81.7 jit_solution(9894198374751239972)
XLA Ops:
  1.3 78.9 %update.1 = (f32[8,96,256]{2,1,0:T(8,128)S(1)}, f32[96,1024]{1,0:T(8,128)S(1)}, f32[8,128]{1,0:T(8,128)S(1)}) custom-call(f32[1]{0:T(128)S(6)} %copy.7.ridge_ref, s32[8,1024]{1,0:T(8,128)} %bitcast.6, bf16[1024]{0:T(1024)(128)(2,1)} %weights_ref.1, f32[96,1024]{1,0:T(8,128)} %bitcast.5), custom_call_target="tpu_custom_call" | custom-call | tf_op jit(solution)/shard_map/update/pallas_call | solution.py:448
  80.2 1.5 %store.1 = (f32[8,96,256]{2,1,0:T(8,128)}, f32[96,1024]{1,0:T(8,128)}, f32[1,1]{1,0:T(1,128)}) custom-call(f32[8,96,256]{2,1,0:T(8,128)S(1)} %get-tuple-element.9.books_ref, f32[96,1024]{1,0:T(8,128)S(1)} %get-tuple-element.10.residual_ref, f32[8,128]{1,0:T(8,128)S(1)} %get-tuple-element.11.sum_ref), custom_call_target="tpu_custom_call" | custom-call | tf_op jit(solution)/shard_map/store/pallas_call | solution.py:496
